TPU v7x, 512 devices: a whole 4x4x16 slice. The times are simulated.
512 devices in a mesh: pages: 128 (over x, z, core), queries: 4 (over y).
Axes of the slice: x: 4, y: 4, z: 16, core: 2. Of those that a mesh axis runs over, the one named last changes fastest.
Arguments:
- query_tokens: bfloat16 [128, 32, 128], P('pages'), may hold values from -1 to 1
- page_patches: bfloat16 [256, 1536, 128], P('pages', 'queries'), may hold values from -1 to 1, as said below
- patch_counts: int32 [256], P('pages'), may hold values from 512 to 1536, as said below
- positive_page: int32 [128], replicated, may hold values from 0 to 255
Outputs:
- query_loss: float32 [128], replicated
- query_grad: float32 [128, 32, 128], P('pages', 'queries')
- page_grad: float32 [256, 1536, 128], P('pages', 'queries')
Inputs may be any that keep to these rules, and one draw needn't show every extreme that they name: `patch_counts`: each page's number of valid patches; some page has exactly 1536. `page_patches`: slots at or past a page's count hold arbitrary values.
All inputs are finite; a program needn't handle non-finite values.
Results may differ from a plain program's by a relative error of at most 0.0028.
Values may be sent and summed in bfloat16 or wider, within the bound.
A program may use at most 64 MiB of HBM per device.

v0:
```python
import jax
import jax.numpy as jnp
from jax import lax
from jax.sharding import PartitionSpec as P

smooth_tau = 0.05
page_temp = 0.02
neg_large = -1e30


def combined_all(part, axis, combine):
    gathered = jax.tree.map(lambda a: lax.all_gather(a, axis), part)

    def take(source):
        return jax.tree.map(lambda a: lax.dynamic_index_in_dim(a, source, 0, False), gathered)

    return lax.fori_loop(
        1, lax.axis_size(axis), lambda source, state: combine(state, take(source)), take(0)
    )


def merge_patch(first, second):
    highest = jnp.maximum(first[0], second[0])
    run_total = first[1] * jnp.exp((first[0] - highest) / smooth_tau) + second[1] * jnp.exp(
        (second[0] - highest) / smooth_tau
    )
    return (highest, run_total)


def merge_page(first, second):
    highest = jnp.maximum(first[0], second[0])
    run_total = first[1] * jnp.exp(first[0] - highest) + second[1] * jnp.exp(second[0] - highest)
    return (highest, run_total, first[2] + second[2])


def shards(query_tokens, page_patches, patch_counts, positive_page):
    group_slot = lax.axis_index("queries")
    gathered = lax.all_gather(query_tokens, "pages", axis=0, tiled=True)
    query_count, query_len, embed_width = gathered.shape
    token_rows = gathered.reshape(query_count * query_len, embed_width)
    row_total = token_rows.shape[0]
    block_rows = min(2048, row_total)
    block_count = row_total // block_rows
    page_local, patch_local, _ = page_patches.shape
    tile_rows = min(128, patch_local)
    live_rows = jnp.clip(patch_counts - group_slot * patch_local, 0, patch_local)
    tile_count = (live_rows + tile_rows - 1) // tile_rows
    tile_pos = jnp.arange(tile_rows, dtype=jnp.int32)

    def tile_scores(block_tokens, page_slab, live_count, tile_idx):
        row_start = tile_idx * tile_rows
        patch_tile = lax.dynamic_slice_in_dim(page_slab, row_start, tile_rows, 0)
        valid_mask = row_start + tile_pos < live_count
        similar = jnp.einsum(
            "re,pe->rp", block_tokens, patch_tile, preferred_element_type=jnp.float32
        )
        return (patch_tile, valid_mask, jnp.where(valid_mask[None, :], similar, neg_large))

    highest_list = []
    total_list = []
    score_list = []
    for page_idx in range(page_local):
        page_slab = page_patches[page_idx]
        live_count = live_rows[page_idx]
        steps_here = tile_count[page_idx]

        def forward_block(block_idx, loop_state):
            highest, run_total, score_page = loop_state
            offset = block_idx * block_rows
            block_tokens = lax.dynamic_slice_in_dim(token_rows, offset, block_rows, 0)

            def forward_tile(tile_idx, inner_state):
                run_max, run_sum, score_buf = inner_state
                _, valid_mask, masked = tile_scores(block_tokens, page_slab, live_count, tile_idx)
                new_max = jnp.maximum(run_max, jnp.max(masked, axis=1))
                fresh_terms = jnp.where(
                    valid_mask[None, :], jnp.exp((masked - new_max[:, None]) / smooth_tau), 0.0
                )
                new_sum = run_sum * jnp.exp((run_max - new_max) / smooth_tau) + jnp.sum(
                    fresh_terms, axis=1
                )
                return (new_max, new_sum, score_buf)

            start_state = (
                jnp.full((block_rows,), neg_large, jnp.float32),
                jnp.zeros((block_rows,), jnp.float32),
                score_page,
            )
            run_max, run_sum, score_page = lax.fori_loop(0, steps_here, forward_tile, start_state)
            highest = lax.dynamic_update_slice_in_dim(highest, run_max, offset, 0)
            run_total = lax.dynamic_update_slice_in_dim(run_total, run_sum, offset, 0)
            return (highest, run_total, score_page)

        score_start = jnp.zeros((1, 1), jnp.float32)
        start_page = (
            jnp.full((row_total,), neg_large, jnp.float32),
            jnp.zeros((row_total,), jnp.float32),
            score_start,
        )
        highest, run_total, score_page = lax.fori_loop(0, block_count, forward_block, start_page)
        highest_list.append(highest)
        total_list.append(run_total)
        score_list.append(score_page)
    highest, run_total = combined_all(
        (jnp.stack(highest_list), jnp.stack(total_list)), "queries", merge_patch
    )
    patch_lse = highest + smooth_tau * jnp.log(run_total)
    smooth = patch_lse - smooth_tau * jnp.log(patch_counts.astype(jnp.float32))[:, None]
    logits = smooth.reshape(page_local, query_count, query_len).sum(axis=2) / page_temp
    page_ids = lax.axis_index("pages") * page_local + jnp.arange(page_local, dtype=jnp.int32)
    is_positive = page_ids[:, None] == positive_page[None, :]
    local_max = jnp.max(logits, axis=0)
    local_sum = jnp.sum(jnp.exp(logits - local_max[None, :]), axis=0)
    local_pos = jnp.sum(jnp.where(is_positive, logits, 0.0), axis=0)
    page_max, page_sum, page_pos = combined_all(
        (local_max, local_sum, local_pos), "pages", merge_page
    )
    query_loss = page_max + jnp.log(page_sum) - page_pos
    weights = (
        jnp.exp(logits - page_max[None, :]) / page_sum[None, :] - is_positive.astype(jnp.float32)
    ) / page_temp
    row_weights = jnp.broadcast_to(
        weights[:, :, None], (page_local, query_count, query_len)
    ).reshape(page_local, row_total)
    grad_rows = jnp.zeros((row_total, embed_width), jnp.float32)
    grad_list = []
    for page_idx in range(page_local):
        page_slab = page_patches[page_idx]
        live_count = live_rows[page_idx]
        steps_here = tile_count[page_idx]
        page_lse = patch_lse[page_idx]
        page_weight = row_weights[page_idx]
        score_page = score_list[page_idx]

        def backward_block(block_idx, loop_state):
            grad_all, grad_slab = loop_state
            offset = block_idx * block_rows
            block_tokens = lax.dynamic_slice_in_dim(token_rows, offset, block_rows, 0)
            block_lse = lax.dynamic_slice_in_dim(page_lse, offset, block_rows, 0)
            block_weight = lax.dynamic_slice_in_dim(page_weight, offset, block_rows, 0)

            def backward_tile(tile_idx, inner_state):
                grad_block, slab_grad = inner_state
                row_start = tile_idx * tile_rows
                patch_tile, valid_mask, masked = tile_scores(
                    block_tokens, page_slab, live_count, tile_idx
                )
                prob_tile = jnp.where(
                    valid_mask[None, :], jnp.exp((masked - block_lse[:, None]) / smooth_tau), 0.0
                )
                coef_tile = (block_weight[:, None] * prob_tile).astype(jnp.bfloat16)
                grad_block = grad_block + jnp.dot(
                    coef_tile, patch_tile, preferred_element_type=jnp.float32
                )
                tile_grad = jnp.einsum(
                    "rp,re->pe", coef_tile, block_tokens, preferred_element_type=jnp.float32
                )
                current = lax.dynamic_slice_in_dim(slab_grad, row_start, tile_rows, 0)
                slab_grad = lax.dynamic_update_slice_in_dim(
                    slab_grad, current + tile_grad, row_start, 0
                )
                return (grad_block, slab_grad)

            grad_block = lax.dynamic_slice_in_dim(grad_all, offset, block_rows, 0)
            grad_block, grad_slab = lax.fori_loop(
                0, steps_here, backward_tile, (grad_block, grad_slab)
            )
            grad_all = lax.dynamic_update_slice_in_dim(grad_all, grad_block, offset, 0)
            return (grad_all, grad_slab)

        start_slab = jnp.zeros((patch_local, embed_width), jnp.float32)
        grad_rows, grad_slab = lax.fori_loop(
            0, block_count, backward_block, (grad_rows, start_slab)
        )
        grad_list.append(grad_slab)
    grad_work = jnp.stack(grad_list)
    grad_three = grad_rows.reshape(query_count, query_len, embed_width)
    partial_value = lax.psum_scatter(grad_three, "pages", scatter_dimension=0, tiled=True)
    query_grad = lax.psum_scatter(partial_value, "queries", scatter_dimension=1, tiled=True)
    return (query_loss, query_grad, grad_work)


def solution(mesh):
    in_specs = (P("pages", None, None), P("pages", "queries", None), P("pages"), P())
    out_specs = (P(), P("pages", "queries", None), P("pages", "queries", None))
    return jax.shard_map(shards, mesh=mesh, in_specs=in_specs, out_specs=out_specs, check_vma=False)
```

profile of v0, /device:TPU:2, one launch (start us, length us, event | category | flops | bytes accessed | tf_op | source)
XLA Modules:
  0.0 752.8 jit_solution(8003784564789250477)
XLA Ops:
  10.9 135.5 %all-gather.12.cloned.1.call-done = bf16[128,32,128]{2,1,0:T(8,128)(2,1)} async-done(((bf16[1,32,128]{2,1,0:T(8,128)(2,1)}), bf16[128,32,128]{2,1,0:T(8,128)(2,1)}) %all-gather.12.cloned.1.call-update) | async-done | bytes 1048592 | tf_op jit(solution)/shard_map/all_gather | solution.py:38
  146.5 16.4 %while.217 = (s32[]{:T(128)}, f32[4096]{0:T(1024)S(1)}, f32[4096]{0:T(1024)S(1)}, bf16[4096,128]{1,0:T(8,128)(2,1)}, s32[]{:T(128)}, /*index=5*/s32[]{:T(128)}, ...) while((s32[]{:T(128)}, f32[4096]{0:T(1024)S(1)}, ...), condition=%wide.region_11.12_spmd.clone, body=%wide.region_6.11_spmd.clone.sunk | while | flops 68688144 | bytes 3860742 | solution.py:100
  147.6 6.5 while.223
  155.8 6.5 while.223
  162.9 15.9 %while.215 = (s32[]{:T(128)}, f32[4096]{0:T(1024)S(1)}, f32[4096]{0:T(1024)S(1)}, bf16[4096,128]{1,0:T(8,128)(2,1)}, s32[]{:T(128)}, /*index=5*/s32[]{:T(128)}, ...) while((s32[]{:T(128)}, f32[4096]{0:T(1024)S(1)}, ...), condition=%wide.region_5.6_spmd.clone, body=%wide.region_0.5_spmd.clone.sunk | while | flops 68688144 | bytes 3860742 | solution.py:100
  164.1 6.2 while.222
  172.0 6.2 while.222
  178.8 12.0 %all-gather.5 = f32[4,2,4096]{2,1,0:T(2,128)S(1)} all-gather(f32[1,2,4096]{2,1,0:T(2,128)S(1)} %maximum_bitcast_fusion), channel_id=2, replica_groups=mesh['pages'=128,'queries'=4] {'queries'}, dimensions={0}, use_global_device_ids=true | all-gather | bytes 163840 | tf_op jit(solution)/shard_map/all_gather | solution.py:12
  190.9 12.0 %all-gather.6 = f32[4,2,4096]{2,1,0:T(2,128)S(1)} all-gather(f32[1,2,4096]{2,1,0:T(2,128)S(1)} %maximum_bitcast_fusion.1), channel_id=3, replica_groups=mesh['pages'=128,'queries'=4] {'queries'}, dimensions={0}, use_global_device_ids=true | all-gather | bytes 163840 | tf_op jit(solution)/shard_map/all_gather | solution.py:12
  203.6 73.3 %all-gather.7 = f32[128,1,128]{2,1,0:T(1,128)S(1)} all-gather(f32[1,1,128]{2,1,0:T(1,128)S(1)} %bitcast.124), channel_id=4, replica_groups=mesh['pages'=128,'queries'=4] {'pages'}, dimensions={0}, use_global_device_ids=true | all-gather | bytes 66048 | tf_op jit(solution)/shard_map/all_gather | solution.py:12
  276.9 72.8 %all-gather.8 = f32[128,1,128]{2,1,0:T(1,128)S(1)} all-gather(f32[1,1,128]{2,1,0:T(1,128)S(1)} %bitcast.127), channel_id=5, replica_groups=mesh['pages'=128,'queries'=4] {'pages'}, dimensions={0}, use_global_device_ids=true | all-gather | bytes 66048 | tf_op jit(solution)/shard_map/all_gather | solution.py:12
  349.7 72.7 %all-gather.9 = f32[128,1,128]{2,1,0:T(1,128)S(1)} all-gather(f32[1,1,128]{2,1,0:T(1,128)S(1)} %bitcast.126), channel_id=6, replica_groups=mesh['pages'=128,'queries'=4] {'pages'}, dimensions={0}, use_global_device_ids=true | all-gather | bytes 66048 | tf_op jit(solution)/shard_map/all_gather | solution.py:12
  422.5 6.1 while.213
  428.8 1.5 broadcast_in_dim.108
  430.3 20.6 %while.219 = (s32[]{:T(128)}, f32[4096,128]{1,0:T(8,128)}, f32[384,128]{1,0:T(8,128)S(1)}, bf16[4096,128]{1,0:T(8,128)(2,1)S(1)}, f32[4096]{0:T(1024)S(1)}, /*in...) while((s32[]{:T(128)}, f32[4096,128]{1,0:T(8,128)}, ...), condition=%wide.region_23.24_spmd.clone, body=%wide.region_20.23_spmd.clone.sunk | while | flops 203178240 | bytes 10209454 | solution.py:172
  430.3 1.3 constant_dynamic-slice_fusion.18
  431.7 7.8 %while.224 = (s32[]{:T(128)}, f32[2048,128]{1,0:T(8,128)S(1)}, f32[384,128]{1,0:T(8,128)S(1)}, s32[]{:T(128)}, f32[2048]{0:T(1024)S(1)}, /*index=5*/s32[128]{0:T...) while((s32[]{:T(128)}, f32[2048,128]{1,0:T(8,128)S(1)}, ...), condition=%wide.region_22.22_spmd, body=%wide.region_21.21_spmd.sunk | while | flops 203178240 | bytes 4932943 | solution.py:165
  442.0 7.8 %while.224 = (s32[]{:T(128)}, f32[2048,128]{1,0:T(8,128)S(1)}, f32[384,128]{1,0:T(8,128)S(1)}, s32[]{:T(128)}, f32[2048]{0:T(1024)S(1)}, /*index=5*/s32[128]{0:T...) while((s32[]{:T(128)}, f32[2048,128]{1,0:T(8,128)S(1)}, ...), condition=%wide.region_22.22_spmd, body=%wide.region_21.21_spmd.sunk | while | flops 203178240 | bytes 4932943 | solution.py:165
  451.1 21.1 %while.221 = (s32[]{:T(128)}, f32[4096,128]{1,0:T(8,128)}, f32[384,128]{1,0:T(8,128)S(1)}, bf16[4096,128]{1,0:T(8,128)(2,1)S(1)}, f32[4096]{0:T(1024)S(1)}, /*in...) while((s32[]{:T(128)}, f32[4096,128]{1,0:T(8,128)}, ...), condition=%wide.region_27.28_spmd.clone, body=%wide.region_24.27_spmd.clone.sunk | while | flops 203178240 | bytes 10209454 | solution.py:172
  451.1 1.3 constant_dynamic-slice_fusion.20
  452.5 8.1 %while.225 = (s32[]{:T(128)}, f32[2048,128]{1,0:T(8,128)S(1)}, f32[384,128]{1,0:T(8,128)S(1)}, s32[]{:T(128)}, f32[2048]{0:T(1024)S(1)}, /*index=5*/s32[128]{0:T...) while((s32[]{:T(128)}, f32[2048,128]{1,0:T(8,128)S(1)}, ...), condition=%wide.region_26.26_spmd, body=%wide.region_25.25_spmd.sunk | while | flops 203178240 | bytes 4932943 | solution.py:165
  463.0 8.1 %while.225 = (s32[]{:T(128)}, f32[2048,128]{1,0:T(8,128)S(1)}, f32[384,128]{1,0:T(8,128)S(1)}, s32[]{:T(128)}, f32[2048]{0:T(1024)S(1)}, /*index=5*/s32[128]{0:T...) while((s32[]{:T(128)}, f32[2048,128]{1,0:T(8,128)S(1)}, ...), condition=%wide.region_26.26_spmd, body=%wide.region_25.25_spmd.sunk | while | flops 203178240 | bytes 4932943 | solution.py:165
  475.5 252.4 %reduce-scatter.3.cloned.1.call-done = f32[1,32,128]{2,1,0:T(8,128)} async-done(((f32[128,32,128]{2,1,0:T(8,128)}), f32[1,32,128]{2,1,0:T(8,128)}) %reduce-scatter.3.cloned.1.call-update) | async-done | bytes 16400 | tf_op jit(solution)/shard_map/reduce_scatter | solution.py:178
  727.9 17.5 %all-reduce = f32[1,32,128]{2,1,0:T(8,128)S(1)} all-reduce(f32[1,32,128]{2,1,0:T(8,128)} %reduce-scatter.3.cloned.1.call-done), channel_id=8, replica_groups=mesh['pages'=128,'queries'=4] {'queries'}, use_global_device_ids=true, to_apply=%region_29.30.clone | all-reduce | flops 4096 | bytes 32768
  (339 shorter events, 60.1 us)
Async XLA Ops:
  7.2 139.3 %all-gather.12.cloned.1.call-start = ((), (), s32[]{:S(2)}) async-start(), calls=%async_computation.1 | async-start | bytes 1056768 | tf_op jit(solution)/shard_map/all_gather | solution.py:38
  7.9 720.0 %reduce-scatter.3.cloned.1.call-start = ((), (), s32[]{:S(2)}) async-start(), calls=%async_computation.2 | async-start | bytes 2113536 | tf_op jit(solution)/shard_map/reduce_scatter | solution.py:178
  178.8 24.7 %copy-start.1 = (s32[128]{0:T(128)S(1)}, s32[128]{0:T(128)}, u32[]{:S(2)}) copy-start(s32[128]{0:T(128)} %param.27) | copy-start | bytes 1540
  202.9 227.4 %copy-start = (bf16[4096,128]{1,0:T(8,128)(2,1)S(1)}, bf16[4096,128]{1,0:T(8,128)(2,1)}, u32[]{:S(2)}) copy-start(bf16[4096,128]{1,0:T(8,128)(2,1)} %get-tuple-element.2438) | copy-start | bytes 3145732
Sparse Core Ops, SparseCore 0:
  10.9 135.4 all-gather.11
  472.4 255.4 reduce-scatter.2
where the time goes:
time: 754 us; the launch traced here: 753 us
  waiting for transfers between devices  389 us (52%)
  blocking collectives  260 us (34%)
  loops' own time  25.9 us (3%)
  other arithmetic  24.1 us (3%)
  local copies, waits for them, and re-layouts  22 us (3%)
  matrix products  16.9 us (2%)
  between operations  14.8 us (2%)
    reduce_scatter x1, waiting for transfers between devices, shards(): lax.psum_scatter(grad_three, 'pages', scatter_dimension=0, tiled=True)  252 us
    all_gather x5, blocking collectives, combined_all(): gathered = jax.tree.map(lambda a: lax.all_gather(a, axis), part)  243 us
    all_gather x1, waiting for transfers between devices, shards(): gathered = lax.all_gather(query_tokens, 'pages', axis=0, tiled=True)  136 us
    unnamed x1, blocking collectives  17.5 us
  transfers between devices with their start and end apart: 2, of which 2 were waited for; matrix products, arithmetic and copies ran while one was open for 1% of the time, Pallas kernels for 0%

commit v1 on v0

--- a/solution.py
+++ b/solution.py
@@ -35,7 +35,9 @@
 
 def shards(query_tokens, page_patches, patch_counts, positive_page):
     group_slot = lax.axis_index("queries")
-    gathered = lax.all_gather(query_tokens, "pages", axis=0, tiled=True)
+    gathered = jnp.concatenate(
+        lax.all_to_all(jnp.stack([query_tokens] * lax.axis_size("pages")), "pages", 0, 0), axis=0
+    )
     query_count, query_len, embed_width = gathered.shape
     token_rows = gathered.reshape(query_count * query_len, embed_width)
     row_total = token_rows.shape[0]

time: 754 us -> 686 us (0.910)
  the two profiles are of different devices: /device:TPU:2 before, /device:TPU:4 now
where the time goes in v1:
time: 686 us; the launch traced here: 685 us
  waiting for transfers between devices  309 us (45%)
  blocking collectives  259 us (38%)
  loops' own time  24 us (3%)
  other arithmetic  23.5 us (3%)
  starting transfers between devices  19.8 us (3%)
  local copies, waits for them, and re-layouts  18.8 us (3%)
  matrix products  17 us (2%)
  between operations  14.8 us (2%)
    reduce_scatter x1, waiting for transfers between devices, shards(): lax.psum_scatter(grad_three, 'pages', scatter_dimension=0, tiled=True)  254 us
    all_gather x5, blocking collectives, combined_all(): gathered = jax.tree.map(lambda a: lax.all_gather(a, axis), part)  241 us
    all_to_all x1, waiting for transfers between devices, shards(): lax.all_to_all(jnp.stack([query_tokens] * lax.axis_size('pages')), 'pages...  54.6 us
    all_to_all x1, starting transfers between devices, shards(): lax.all_to_all(jnp.stack([query_tokens] * lax.axis_size('pages')), 'pages...  19.7 us
    unnamed x1, blocking collectives  17.5 us
    lt x24, other arithmetic, tile_scores(): valid_mask = row_start + tile_pos < live_count  14.8 us
  transfers between devices with their start and end apart: 2, of which 2 were waited for; matrix products, arithmetic and copies ran while one was open for 0% of the time, Pallas kernels for 0%

profile of v1, /device:TPU:4, one launch (start us, length us, event | category | flops | bytes accessed | tf_op | source)
XLA Modules:
  0.0 685.5 jit_solution(2993079939851853722)
XLA Ops:
  7.2 1.9 stack.20
  9.0 19.7 %all-to-all-start = ((bf16[128,1,32,128]{3,2,1,0:T(8,128)(2,1)}), bf16[128,1,32,128]{3,2,1,0:T(8,128)(2,1)S(1)}, u32[]{:S(2)}, u32[]{:S(2)}) async-start(bf16[128,1,32,128]{3,2,1,0:T(8,128)(2,1)} %stack.20), calls=%async_computation | async-start | bytes 2097152 | tf_op jit(solution)/shard_map/all_to_all | solution.py:39
  29.5 54.6 %all-to-all-done = bf16[128,1,32,128]{3,2,1,0:T(8,128)(2,1)S(1)} async-done(((bf16[128,1,32,128]{3,2,1,0:T(8,128)(2,1)}), bf16[128,1,32,128]{3,2,1,0:T(8,128)(2,1)S(1)}, u32[]{:S(2)}, u32[]{:S(2)}) %all-to-all-start) | async-done | bytes 1048608 | tf_op jit(solution)/shard_map/all_to_all | solution.py:39
  84.2 13.7 %while.217 = (s32[]{:T(128)}, f32[4096]{0:T(1024)S(1)}, f32[4096]{0:T(1024)S(1)}, bf16[4096,128]{1,0:T(8,128)(2,1)S(1)}, s32[]{:T(128)}, /*index=5*/s32[]{:T(128...) while((s32[]{:T(128)}, f32[4096]{0:T(1024)S(1)}, ...), condition=%wide.region_11.12_spmd.clone, body=%wide.region_6.11_spmd.clone.sunk | while | flops 68688144 | bytes 3860742 | solution.py:102
  84.2 6.2 while.223
  91.1 6.2 while.223
  97.9 13.9 %while.215 = (s32[]{:T(128)}, f32[4096]{0:T(1024)S(1)}, f32[4096]{0:T(1024)S(1)}, bf16[4096,128]{1,0:T(8,128)(2,1)S(1)}, s32[]{:T(128)}, /*index=5*/s32[]{:T(128...) while((s32[]{:T(128)}, f32[4096]{0:T(1024)S(1)}, ...), condition=%wide.region_5.6_spmd.clone, body=%wide.region_0.5_spmd.clone.sunk | while | flops 68688144 | bytes 3860742 | solution.py:102
  98.0 6.2 while.222
  105.0 6.2 while.222
  111.8 12.5 %all-gather.5 = f32[4,2,4096]{2,1,0:T(2,128)S(1)} all-gather(f32[1,2,4096]{2,1,0:T(2,128)S(1)} %maximum_bitcast_fusion), channel_id=2, replica_groups=mesh['pages'=128,'queries'=4] {'queries'}, dimensions={0}, use_global_device_ids=true | all-gather | bytes 163840 | tf_op jit(solution)/shard_map/all_gather | solution.py:12
  124.4 12.0 %all-gather.6 = f32[4,2,4096]{2,1,0:T(2,128)S(1)} all-gather(f32[1,2,4096]{2,1,0:T(2,128)S(1)} %maximum_bitcast_fusion.1), channel_id=3, replica_groups=mesh['pages'=128,'queries'=4] {'queries'}, dimensions={0}, use_global_device_ids=true | all-gather | bytes 163840 | tf_op jit(solution)/shard_map/all_gather | solution.py:12
  137.1 71.7 %all-gather.7 = f32[128,1,128]{2,1,0:T(1,128)S(1)} all-gather(f32[1,1,128]{2,1,0:T(1,128)S(1)} %bitcast.126), channel_id=4, replica_groups=mesh['pages'=128,'queries'=4] {'pages'}, dimensions={0}, use_global_device_ids=true | all-gather | bytes 66048 | tf_op jit(solution)/shard_map/all_gather | solution.py:12
  208.8 72.6 %all-gather.8 = f32[128,1,128]{2,1,0:T(1,128)S(1)} all-gather(f32[1,1,128]{2,1,0:T(1,128)S(1)} %bitcast.129), channel_id=5, replica_groups=mesh['pages'=128,'queries'=4] {'pages'}, dimensions={0}, use_global_device_ids=true | all-gather | bytes 66048 | tf_op jit(solution)/shard_map/all_gather | solution.py:12
  281.4 72.3 %all-gather.9 = f32[128,1,128]{2,1,0:T(1,128)S(1)} all-gather(f32[1,1,128]{2,1,0:T(1,128)S(1)} %bitcast.128), channel_id=6, replica_groups=mesh['pages'=128,'queries'=4] {'pages'}, dimensions={0}, use_global_device_ids=true | all-gather | bytes 66048 | tf_op jit(solution)/shard_map/all_gather | solution.py:12
  353.7 6.0 while.213
  360.0 1.5 broadcast_in_dim.108
  361.5 20.7 %while.219 = (s32[]{:T(128)}, f32[4096,128]{1,0:T(8,128)}, f32[384,128]{1,0:T(8,128)S(1)}, bf16[4096,128]{1,0:T(8,128)(2,1)S(1)}, f32[4096]{0:T(1024)S(1)}, /*in...) while((s32[]{:T(128)}, f32[4096,128]{1,0:T(8,128)}, ...), condition=%wide.region_23.24_spmd.clone, body=%wide.region_20.23_spmd.clone.sunk | while | flops 203178240 | bytes 10209454 | solution.py:174
  362.9 7.9 %while.224 = (s32[]{:T(128)}, f32[2048,128]{1,0:T(8,128)S(1)}, f32[384,128]{1,0:T(8,128)S(1)}, s32[]{:T(128)}, f32[2048]{0:T(1024)S(1)}, /*index=5*/s32[128]{0:T...) while((s32[]{:T(128)}, f32[2048,128]{1,0:T(8,128)S(1)}, ...), condition=%wide.region_22.22_spmd, body=%wide.region_21.21_spmd.sunk | while | flops 203178240 | bytes 4932943 | solution.py:167
  373.2 7.8 %while.224 = (s32[]{:T(128)}, f32[2048,128]{1,0:T(8,128)S(1)}, f32[384,128]{1,0:T(8,128)S(1)}, s32[]{:T(128)}, f32[2048]{0:T(1024)S(1)}, /*index=5*/s32[128]{0:T...) while((s32[]{:T(128)}, f32[2048,128]{1,0:T(8,128)S(1)}, ...), condition=%wide.region_22.22_spmd, body=%wide.region_21.21_spmd.sunk | while | flops 203178240 | bytes 4932943 | solution.py:167
  382.4 20.5 %while.221 = (s32[]{:T(128)}, f32[4096,128]{1,0:T(8,128)}, f32[384,128]{1,0:T(8,128)S(1)}, bf16[4096,128]{1,0:T(8,128)(2,1)S(1)}, f32[4096]{0:T(1024)S(1)}, /*in...) while((s32[]{:T(128)}, f32[4096,128]{1,0:T(8,128)}, ...), condition=%wide.region_27.28_spmd.clone, body=%wide.region_24.27_spmd.clone.sunk | while | flops 203178240 | bytes 10209454 | solution.py:174
  383.8 7.8 %while.225 = (s32[]{:T(128)}, f32[2048,128]{1,0:T(8,128)S(1)}, f32[384,128]{1,0:T(8,128)S(1)}, s32[]{:T(128)}, f32[2048]{0:T(1024)S(1)}, /*index=5*/s32[128]{0:T...) while((s32[]{:T(128)}, f32[2048,128]{1,0:T(8,128)S(1)}, ...), condition=%wide.region_26.26_spmd, body=%wide.region_25.25_spmd.sunk | while | flops 203178240 | bytes 4932943 | solution.py:167
  394.0 7.8 %while.225 = (s32[]{:T(128)}, f32[2048,128]{1,0:T(8,128)S(1)}, f32[384,128]{1,0:T(8,128)S(1)}, s32[]{:T(128)}, f32[2048]{0:T(1024)S(1)}, /*index=5*/s32[128]{0:T...) while((s32[]{:T(128)}, f32[2048,128]{1,0:T(8,128)S(1)}, ...), condition=%wide.region_26.26_spmd, body=%wide.region_25.25_spmd.sunk | while | flops 203178240 | bytes 4932943 | solution.py:167
  406.1 254.4 %reduce-scatter.3.cloned.1.call-done = f32[1,32,128]{2,1,0:T(8,128)} async-done(((f32[128,32,128]{2,1,0:T(8,128)}), f32[1,32,128]{2,1,0:T(8,128)}) %reduce-scatter.3.cloned.1.call-update) | async-done | bytes 16400 | tf_op jit(solution)/shard_map/reduce_scatter | solution.py:180
  660.5 17.5 %all-reduce = f32[1,32,128]{2,1,0:T(8,128)S(1)} all-reduce(f32[1,32,128]{2,1,0:T(8,128)} %reduce-scatter.3.cloned.1.call-done), channel_id=8, replica_groups=mesh['pages'=128,'queries'=4] {'queries'}, use_global_device_ids=true, to_apply=%region_29.30.clone | all-reduce | flops 4096 | bytes 32768
  (341 shorter events, 56.2 us)
Async XLA Ops:
  7.2 21.7 %copy-start.2 = (s32[2]{0:T(128)S(1)}, s32[2]{0:T(128)}, u32[]{:S(2)}) copy-start(s32[2]{0:T(128)} %param.26) | copy-start | bytes 28
  7.2 22.3 %copy-start = (bf16[2,384,128]{2,1,0:T(8,128)(2,1)S(1)}, bf16[2,384,128]{2,1,0:T(8,128)(2,1)}, u32[]{:S(2)}) copy-start(bf16[2,384,128]{2,1,0:T(8,128)(2,1)} %param.25) | copy-start | bytes 589828
  9.0 75.1 %all-to-all-start = ((bf16[128,1,32,128]{3,2,1,0:T(8,128)(2,1)}), bf16[128,1,32,128]{3,2,1,0:T(8,128)(2,1)S(1)}, u32[]{:S(2)}, u32[]{:S(2)}) async-start(bf16[128,1,32,128]{3,2,1,0:T(8,128)(2,1)} %stack.20), calls=%async_computation | async-start | bytes 2097152 | tf_op jit(solution)/shard_map/all_to_all | solution.py:39
  28.8 631.8 %reduce-scatter.3.cloned.1.call-start = ((), (), s32[]{:S(2)}) async-start(), calls=%async_computation.2 | async-start | bytes 2113536 | tf_op jit(solution)/shard_map/reduce_scatter | solution.py:180
  111.8 25.2 %copy-start.1 = (s32[128]{0:T(128)S(1)}, s32[128]{0:T(128)}, u32[]{:S(2)}) copy-start(s32[128]{0:T(128)} %param.27) | copy-start | bytes 1540
Sparse Core Ops, SparseCore 0:
  403.0 257.4 reduce-scatter.2
